TPU v7x, 256 devices: a whole 4x4x8 slice. The times are simulated.
256 devices in a mesh: gx: 16 (over z, x_hi), gy: 16 (over y, x_lo, core).
Axes of the slice: x: 4 (x_hi: 2, x_lo: 2; x = x_hi * 2 + x_lo), y: 4, z: 8, core: 2. Of those that a mesh axis runs over, the one named last changes fastest.
Arguments:
- f_in: float32 [19, 16, 256, 2048], P(None, None, 'gx', 'gy')
- rotor_place: int32 [40, 3], replicated, may hold values from 0 to 15, as said below
- marker_cell: int32 [40, 8192], replicated, may hold values from 16384 to 2078527, as said below
- pitch_phase: int32 [40, 2], replicated, may hold values from 0 to 63
- blade_area: float32 [16, 16, 2, 8192], P('gx', 'gy'), may hold values from 0.3 to 1.2
- blade_twist: float32 [16, 16, 2, 8192], P('gx', 'gy'), may hold values from -0.6 to 0.6
- blade_speed: float32 [16, 16, 2, 8192], P('gx', 'gy'), may hold values from 1.5 to 3
- blade_angle: float32 [16, 16, 2, 8192], P('gx', 'gy'), may hold values from -3.14 to 3.14, as said below
- filt_in: float32 [16, 16, 2, 3, 8192], P('gx', 'gy'), may hold values from -1.5 to 1.5
Outputs:
- f_out: float32 [19, 16, 256, 2048], P(None, None, 'gx', 'gy')
- loads_out: float32 [16, 16, 2, 3, 8192], P('gx', 'gy')
- filt_out: float32 [16, 16, 2, 3, 8192], P('gx', 'gy')
Inputs may be any that keep to these rules, and one draw needn't show every extreme that they name: `rotor_place`: column 0 is a streamwise tile holding at most 3 rotors, some exactly 3; column 1 a plane 0 to 15; column 2 the owner's spanwise tile. Every streamwise tile holds 2 or more rotors; one owner holds at most 2 rotors, exactly 2 in every streamwise tile. `marker_cell`: all stencil cells of one rotor lie within two neighbouring spanwise tiles and within levels 0 to 15; a rotor's stencils may cover one or two tiles. `blade_angle`: azimuths in radians.
All inputs are finite; a program needn't handle non-finite values.
Results may differ from a plain program's by a relative error of at most 0.0003.
Values sent between devices are 32-bit elements; how exact they have to be, the bound alone decides.
A program may use at most 128 MiB of HBM per device.

v0:
```python
import math
import jax
import jax.numpy as jnp
import numpy as np
from jax import lax
from jax.sharding import PartitionSpec as P

PHASES = 64
LATTICE_DIRS = np.array(
    [
        [0, 0, 0],
        [1, 0, 0],
        [-1, 0, 0],
        [0, 1, 0],
        [0, -1, 0],
        [0, 0, 1],
        [0, 0, -1],
        [1, 1, 0],
        [-1, -1, 0],
        [1, -1, 0],
        [-1, 1, 0],
        [1, 0, 1],
        [-1, 0, -1],
        [1, 0, -1],
        [-1, 0, 1],
        [0, 1, 1],
        [0, -1, -1],
        [0, 1, -1],
        [0, -1, 1],
    ]
)
OPPOSITE = [0, 2, 1, 4, 3, 6, 5, 8, 7, 10, 9, 12, 11, 14, 13, 16, 15, 18, 17]
LATTICE_WEIGHTS = np.array([1.0 / 3.0] + [1.0 / 18.0] * 6 + [1.0 / 36.0] * 12)
OMEGA = 1.0 / 0.6
SPREAD = 0.01
MIX = 0.5
PITCH_AMP = 0.2


def extended(block, sides, width):
    for axis, dim in sides:
        count = lax.axis_size(axis)
        forward = [(i, i + 1) for i in range(count - 1)]
        forward.append((count - 1, 0))
        backward = [(target, source) for source, target in forward]
        low = lax.ppermute(
            lax.slice_in_dim(block, block.shape[dim] - width, None, axis=dim), axis, forward
        )
        high = lax.ppermute(lax.slice_in_dim(block, 0, width, axis=dim), axis, backward)
        block = jnp.concatenate([low, block, high], axis=dim)
    return block


def peskin(offsets):
    distance = jnp.abs(offsets)
    near_arg = jnp.maximum(1.0 + 4.0 * distance - 4.0 * distance * distance, 1.0)
    far_arg = jnp.maximum(-7.0 + 12.0 * distance - 4.0 * distance * distance, 1.0)
    near_part = (3.0 - 2.0 * distance + jnp.sqrt(near_arg)) / 8.0
    far_part = (5.0 - 2.0 * distance - jnp.sqrt(far_arg)) / 8.0
    return jnp.where(distance <= 1.0, near_part, far_part)


def dense_rows(anchor, weights, width, start):
    column = jnp.arange(width, dtype=jnp.int32)[None, :] + start
    gap = column - anchor[:, None]
    summed = jnp.zeros(gap.shape, jnp.float32)
    for corner in range(4):
        summed = summed + jnp.where(gap == corner, weights[corner][:, None], 0.0)
    return summed


def stencil_tables(cell_codes, levels, width, start):
    fraction_z = (cell_codes % 8).astype(jnp.float32) / 8.0
    fraction_y = (cell_codes // 8 % 8).astype(jnp.float32) / 8.0
    cell_z = cell_codes // 64 % levels
    cell_y = cell_codes // (64 * levels)
    weights_y = [peskin(corner - 1.0 - fraction_y) for corner in range(4)]
    weights_z = [peskin(corner - 1.0 - fraction_z) for corner in range(4)]
    across = dense_rows(cell_y, weights_y, width, start)
    upward = dense_rows(cell_z, weights_z, levels, jnp.int32(0))
    return (across, upward)


def sample_section(section, across, upward):
    levels = section.shape[1]
    width = section.shape[2]
    flattened = jnp.transpose(section, (2, 0, 1)).reshape(width, 3 * levels)
    partial_value = jnp.dot(
        across, flattened, precision=lax.Precision.HIGHEST, preferred_element_type=jnp.float32
    )
    partial_value = partial_value.reshape(across.shape[0], 3, levels)
    return jnp.transpose(jnp.sum(partial_value * upward[:, None, :], axis=2))


def spread_section(marker_loads, across, upward):
    markers = upward.shape[0]
    levels = upward.shape[1]
    weighted = (upward[:, None, :] * jnp.transpose(marker_loads)[:, :, None]).reshape(
        markers, 3 * levels
    )
    section = lax.dot_general(
        weighted,
        across,
        (((0,), (0,)), ((), ())),
        precision=lax.Precision.HIGHEST,
        preferred_element_type=jnp.float32,
    )
    return -SPREAD * section.reshape(3, levels, across.shape[1])


def pitch_angles(phases):
    return PITCH_AMP * jnp.sin(2.0 * math.pi * phases.astype(jnp.float32) / PHASES)


def blade_loads(filtered, area, twist, speed, angle, pitch):
    axial_speed = filtered[..., 0, :]
    sin_t = jnp.sin(angle)
    cos_t = jnp.cos(angle)
    tangent = speed + sin_t * filtered[..., 1, :] - cos_t * filtered[..., 2, :]
    square = axial_speed * axial_speed + tangent * tangent
    magnitude = jnp.sqrt(square)
    sin_p = axial_speed / magnitude
    cos_p = tangent / magnitude
    blade_pitch = twist + pitch
    sin_a = sin_p * jnp.cos(blade_pitch) - cos_p * jnp.sin(blade_pitch)
    cos_a = cos_p * jnp.cos(blade_pitch) + sin_p * jnp.sin(blade_pitch)
    lift_coef = 2.0 * math.pi * sin_a * cos_a
    drag_coef = 0.02 + sin_a * sin_a
    dynamic = 0.5 * area * square
    normal = dynamic * (lift_coef * cos_p + drag_coef * sin_p)
    tangential = dynamic * (lift_coef * sin_p - drag_coef * cos_p)
    return jnp.stack([normal, -tangential * sin_t, tangential * cos_t], axis=-2)


def velocity(populations):
    lattice = jnp.asarray(LATTICE_DIRS, jnp.float32)
    density = jnp.sum(populations, axis=0)
    parts = [
        jnp.sum(populations * lattice[:, axis][:, None, None, None], axis=0) / density
        for axis in range(3)
    ]
    return jnp.stack(parts)


def collide(populations, force_field):
    lattice = jnp.asarray(LATTICE_DIRS, jnp.float32)
    weights = jnp.asarray(LATTICE_WEIGHTS, jnp.float32)[:, None, None, None]
    density = jnp.sum(populations, axis=0)
    columns = [lattice[:, axis][:, None, None, None] for axis in range(3)]
    parts = [
        (jnp.sum(populations * columns[axis], axis=0) + 0.5 * force_field[axis]) / density
        for axis in range(3)
    ]
    project = (
        columns[0] * parts[0][None] + columns[1] * parts[1][None] + columns[2] * parts[2][None]
    )
    force_proj = (
        columns[0] * force_field[0][None]
        + columns[1] * force_field[1][None]
        + columns[2] * force_field[2][None]
    )
    speed_sq = parts[0] * parts[0] + parts[1] * parts[1] + parts[2] * parts[2]
    work_rate = parts[0] * force_field[0] + parts[1] * force_field[1] + parts[2] * force_field[2]
    equilibrium = (
        weights
        * density[None]
        * (1.0 + 3.0 * project + 4.5 * project * project - 1.5 * speed_sq[None])
    )
    source = (
        (1.0 - 0.5 * OMEGA)
        * weights
        * (3.0 * (force_proj - work_rate[None]) + 9.0 * project * force_proj)
    )
    return populations - OMEGA * (populations - equilibrium) + source


def stream(padded, collided):
    x_cells = collided.shape[2]
    y_cells = collided.shape[3]
    outgoing = []
    for direction in range(19):
        shift_x = int(LATTICE_DIRS[direction, 0])
        shift_y = int(LATTICE_DIRS[direction, 1])
        shift_z = int(LATTICE_DIRS[direction, 2])
        pulled = padded[
            direction, :, 1 - shift_x : 1 - shift_x + x_cells, 1 - shift_y : 1 - shift_y + y_cells
        ]
        mirror = collided[OPPOSITE[direction]]
        if shift_z == 1:
            pulled = jnp.concatenate([mirror[:1], pulled[:-1]], axis=0)
        elif shift_z == -1:
            pulled = jnp.concatenate([pulled[1:], mirror[-1:]], axis=0)
        outgoing.append(pulled)
    return jnp.stack(outgoing)


def with_ghosts(collided):
    padded = extended(collided, (("gx", 2), ("gy", 3)), 1)
    return padded


def local(
    f_in,
    rotor_place,
    marker_cell,
    pitch_phase,
    blade_area,
    blade_twist,
    blade_speed,
    blade_angle,
    filt_in,
):
    levels = f_in.shape[1]
    x_cells = f_in.shape[2]
    y_cells = f_in.shape[3]
    rotors = rotor_place.shape[0]
    step_count = pitch_phase.shape[1]
    owned_count = filt_in.shape[2]
    spread_x = lax.axis_size("gx")
    row_slots = (rotors + spread_x - 1) // spread_x
    here_x = lax.axis_index("gx")
    here_y = lax.axis_index("gy")
    street = rotor_place[:, 0]
    plane_x = rotor_place[:, 1]
    owner_y = rotor_place[:, 2]
    rotor_ids = jnp.arange(rotors, dtype=jnp.int32)
    earlier = rotor_ids[None, :] < rotor_ids[:, None]
    same_row = street[:, None] == street[None, :]
    row_rank = jnp.sum((earlier & same_row).astype(jnp.int32), axis=1)
    same_owner = same_row & (owner_y[:, None] == owner_y[None, :])
    owner_rank = jnp.sum((earlier & same_owner).astype(jnp.int32), axis=1)
    slot_ids = jnp.arange(row_slots, dtype=jnp.int32)
    slot_pick = ((street[None, :] == here_x) & (row_rank[None, :] == slot_ids[:, None])).astype(
        jnp.int32
    )
    slot_valid = jnp.sum(slot_pick, axis=1)
    slot_rotor = jnp.sum(slot_pick * rotor_ids[None, :], axis=1)
    slot_codes = jnp.take(marker_cell, slot_rotor, axis=0)
    slot_plane = jnp.take(plane_x, slot_rotor)
    slot_pitch = pitch_angles(jnp.take(pitch_phase, slot_rotor, axis=0))
    owned_here = (jnp.take(owner_y, slot_rotor) == here_y) & (slot_valid > 0)
    owned_ids = jnp.arange(owned_count, dtype=jnp.int32)
    own_pick = (
        owned_here[None, :] & (jnp.take(owner_rank, slot_rotor)[None, :] == owned_ids[:, None])
    ).astype(jnp.float32)
    valid_float = slot_valid.astype(jnp.float32)
    start_y = here_y * y_cells
    tables = []
    for slot_index in range(row_slots):
        across, upward = stencil_tables(slot_codes[slot_index], levels, y_cells, start_y)
        tables.append((across * valid_float[slot_index], upward))
    x_ids = jnp.arange(x_cells, dtype=jnp.int32)
    filtered = filt_in[0, 0]
    own_pitch = jnp.sum(own_pick[:, :, None] * slot_pitch[None], axis=1)
    populations = f_in
    for step_index in range(step_count):
        field_speed = velocity(populations)
        samples = jnp.stack(
            [
                sample_section(
                    lax.dynamic_index_in_dim(
                        field_speed, slot_plane[slot_index], 2, keepdims=False
                    ),
                    tables[slot_index][0],
                    tables[slot_index][1],
                )
                for slot_index in range(row_slots)
            ]
        )
        sampled = lax.psum(samples, "gy")
        own_sampled = jnp.sum(own_pick[:, :, None, None] * sampled[None], axis=1)
        filtered = filtered + MIX * (own_sampled - filtered)
        own_loads = blade_loads(
            filtered,
            blade_area[0, 0],
            blade_twist[0, 0],
            blade_speed[0, 0],
            blade_angle[0, 0],
            own_pitch[:, step_index][:, None],
        )
        row_loads = jnp.sum(own_pick[:, :, None, None] * own_loads[:, None], axis=0)
        load_rows = lax.psum(row_loads, "gy")
        force_field = jnp.zeros((3, levels, x_cells, y_cells), jnp.float32)
        for slot_index in range(row_slots):
            section = spread_section(
                load_rows[slot_index], tables[slot_index][0], tables[slot_index][1]
            )
            plane_mask = (x_ids == slot_plane[slot_index]).astype(jnp.float32)
            force_field = force_field + section[:, :, None, :] * plane_mask[None, None, :, None]
        collided = collide(populations, force_field)
        populations = stream(with_ghosts(collided), collided)
    has_rotor = jnp.sum(own_pick, axis=1)[:, None, None]
    loads_out = own_loads * has_rotor
    filt_out = filtered * has_rotor
    return (populations, loads_out[None, None], filt_out[None, None])


def solution(mesh):
    in_specs = (
        P(None, None, "gx", "gy"),
        P(),
        P(),
        P(),
        P("gx", "gy", None, None),
        P("gx", "gy", None, None),
        P("gx", "gy", None, None),
        P("gx", "gy", None, None),
        P("gx", "gy", None, None, None),
    )
    out_specs = (
        P(None, None, "gx", "gy"),
        P("gx", "gy", None, None, None),
        P("gx", "gy", None, None, None),
    )
    return jax.shard_map(local, mesh=mesh, in_specs=in_specs, out_specs=out_specs, check_vma=False)
```

profile of v0, /device:TPU:27, one launch (start us, length us, event | category | flops | bytes accessed | tf_op | source)
XLA Modules:
  0.0 818.9 jit_solution(7639344466328767253)
XLA Ops:
  20.0 2.4 multiply_reduce_fusion.5
  23.2 16.3 %fusion.50 = f32[8192,3]{0,1:T(4,128)S(1)} fusion(f32[3,16,128]{2,1,0:T(8,128)S(1)} %bitcast.602, f32[]{:T(128)} %bitcast.34, f32[8192]{0:T(1024)S(1)} %get-tuple-element.179, f32[8192]{0:T(1024)S(1)} %get-tuple-element.178, f32[8192]{0:T(1024)S(1)} %get-tuple-element.177, f32[8192]{0:T(1024)S(1)} %get-tuple-element.175, s32[8192]{0:T(1024)S(1)} %get-tuple-element.170, ...), kind=kOutput, calls=%fused_computation.82 | convolution fusion | flops 618373120 | bytes 811524 | tf_op jit(solution)/shard_map/dot_general | solution.py:88
  39.6 16.2 %fusion.44 = f32[8192,3]{0,1:T(4,128)S(1)} fusion(f32[3,16,128]{2,1,0:T(8,128)S(1)} %bitcast.601, f32[]{:T(128)} %bitcast.8, f32[8192]{0:T(1024)S(1)} %get-tuple-element.157, f32[8192]{0:T(1024)S(1)} %get-tuple-element.156, f32[8192]{0:T(1024)S(1)} %get-tuple-element.155, f32[8192]{0:T(1024)S(1)} %get-tuple-element.153, s32[8192]{0:T(1024)S(1)} %get-tuple-element.148, ...), kind=kOutput, calls=%fused_computation.80 | convolution fusion | flops 618373120 | bytes 811524 | tf_op jit(solution)/shard_map/dot_general | solution.py:88
  56.0 16.4 %fusion.47 = f32[8192,3]{0,1:T(4,128)S(1)} fusion(f32[3,16,128]{2,1,0:T(8,128)S(1)} %bitcast.600, f32[]{:T(128)} %bitcast.23, f32[8192]{0:T(1024)S(1)} %get-tuple-element.168, f32[8192]{0:T(1024)S(1)} %get-tuple-element.167, f32[8192]{0:T(1024)S(1)} %get-tuple-element.166, f32[8192]{0:T(1024)S(1)} %get-tuple-element.164, s32[8192]{0:T(1024)S(1)} %get-tuple-element.159, ...), kind=kOutput, calls=%fused_computation.81 | convolution fusion | flops 618373120 | bytes 811524 | tf_op jit(solution)/shard_map/dot_general | solution.py:88
  76.9 123.3 %all-reduce.5.cloned.1.call-done = f32[3,3,8192]{2,1,0:T(4,128)} async-done(((f32[3,3,8192]{2,1,0:T(4,128)}), f32[3,3,8192]{2,1,0:T(4,128)}) %all-reduce.5.cloned.1.call-update) | async-done | bytes 294928 | tf_op jit(solution)/shard_map/psum | solution.py:270
  200.2 1.5 multiply_reduce_fusion.9
  201.8 1.4 add_multiply_fusion.17
  204.7 1.6 multiply_reduce_fusion.8
  208.5 122.4 %all-reduce.7.cloned.1.call-done = f32[3,3,8192]{2,1,0:T(4,128)} async-done(((f32[3,3,8192]{2,1,0:T(4,128)}), f32[3,3,8192]{2,1,0:T(4,128)}) %all-reduce.7.cloned.1.call-update) | async-done | bytes 294928 | tf_op jit(solution)/shard_map/psum | solution.py:282
  332.0 8.6 %fusion.62 = f32[3,16,128]{2,1,0:T(8,128)S(1)} fusion(f32[]{:T(128)} %bitcast.8, f32[8192]{0:T(1024)} %copy-done.68, f32[8192]{0:T(1024)} %copy-done.66, f32[8192]{0:T(1024)} %copy-done.64, f32[8192]{0:T(1024)S(1)} %copy-done.48, s32[8192]{0:T(1024)S(1)} %get-tuple-element.148, s32[128]{0:T(128)S(1)} %copy-done.120, f32[8192,3]{0,1:T(4,128)S(1)} %get-tuple-element.131, ...), kind=kOutput, calls=%fused_computation.86 | convolution fusion | flops 618010624 | bytes 811524 | tf_op jit(solution)/shard_map/dot_general | solution.py:101
  340.7 7.9 fusion.82
  348.7 8.3 %fusion.72 = f32[3,16,128]{2,1,0:T(8,128)S(1)} fusion(f32[]{:T(128)} %bitcast.23, f32[8192]{0:T(1024)S(1)} %copy-done.77, f32[8192]{0:T(1024)S(1)} %copy-done.74, f32[8192]{0:T(1024)S(1)} %copy-done.71, f32[8192]{0:T(1024)S(1)} %copy-done.54, s32[8192]{0:T(1024)S(1)} %copy-done.51, s32[128]{0:T(128)S(1)} %copy-done.120, ...), kind=kOutput, calls=%fused_computation.88 | convolution fusion | flops 618010624 | bytes 811524 | tf_op jit(solution)/shard_map/dot_general | solution.py:101
  358.7 2.5 fusion.24
  362.1 4.5 collective-permute-start.1
  367.3 1.5 collective-permute-done.1
  368.9 5.5 collective-permute-done
  375.0 4.4 fusion.415
  379.4 4.1 copy.171
  383.5 4.1 copy.169
  387.6 2.3 collective-permute-start.2
  392.2 4.8 collective-permute-done.3
  396.9 5.9 copy.172
  402.8 5.6 copy.170
  408.4 1.9 constant_dynamic-update-slice_fusion.5
  417.6 16.4 %fusion.59 = f32[8192,3]{0,1:T(4,128)S(1)} fusion(f32[3,16,128]{2,1,0:T(8,128)S(1)} %bitcast.605, f32[]{:T(128)} %bitcast.34, f32[8192]{0:T(1024)S(1)} %copy-done.89, f32[8192]{0:T(1024)S(1)} %copy-done.85, f32[8192]{0:T(1024)S(1)} %copy-done.81, f32[8192]{0:T(1024)S(1)} %copy-done.62, s32[8192]{0:T(1024)S(1)} %copy-done.58, s32[128]{0:T(128)S(1)} %copy-done.121, ...), kind=kOutput, calls=%fused_computation.85 | convolution fusion | flops 618373120 | bytes 811524 | tf_op jit(solution)/shard_map/dot_general | solution.py:88
  434.1 16.4 %fusion.56 = f32[8192,3]{0,1:T(4,128)S(1)} fusion(f32[3,16,128]{2,1,0:T(8,128)S(1)} %bitcast.604, f32[]{:T(128)} %bitcast.23, f32[8192]{0:T(1024)S(1)} %copy-done.78, f32[8192]{0:T(1024)S(1)} %copy-done.75, f32[8192]{0:T(1024)S(1)} %copy-done.72, f32[8192]{0:T(1024)S(1)} %copy-done.55, s32[8192]{0:T(1024)S(1)} %copy-done.52, s32[128]{0:T(128)S(1)} %copy-done.121, ...), kind=kOutput, calls=%fused_computation.84 | convolution fusion | flops 618373120 | bytes 811524 | tf_op jit(solution)/shard_map/dot_general | solution.py:88
  450.6 16.3 %fusion.53 = f32[8192,3]{0,1:T(4,128)S(1)} fusion(f32[3,16,128]{2,1,0:T(8,128)S(1)} %bitcast.603, f32[]{:T(128)} %bitcast.8, f32[8192]{0:T(1024)S(1)} %copy-done.69, f32[8192]{0:T(1024)S(1)} %copy-done.67, f32[8192]{0:T(1024)S(1)} %copy-done.65, f32[8192]{0:T(1024)S(1)} %copy-done.49, s32[8192]{0:T(1024)S(1)} %copy-done.46, s32[128]{0:T(128)S(1)} %copy-done.121, ...), kind=kOutput, calls=%fused_computation.83 | convolution fusion | flops 618373120 | bytes 811524 | tf_op jit(solution)/shard_map/dot_general | solution.py:88
  467.9 121.0 %all-reduce.9.cloned.1.call-done = f32[3,3,8192]{2,1,0:T(4,128)} async-done(((f32[3,3,8192]{2,1,0:T(4,128)}), f32[3,3,8192]{2,1,0:T(4,128)}) %all-reduce.9.cloned.1.call-update) | async-done | bytes 294928 | tf_op jit(solution)/shard_map/psum | solution.py:270
  588.9 1.5 multiply_reduce_fusion.7
  590.5 1.6 add_multiply_fusion.15
  593.6 1.6 multiply_reduce_fusion.6
  596.3 123.5 %all-reduce.11.cloned.1.call-done = f32[3,3,8192]{2,1,0:T(4,128)} async-done(((f32[3,3,8192]{2,1,0:T(4,128)}), f32[3,3,8192]{2,1,0:T(4,128)}) %all-reduce.11.cloned.1.call-update) | async-done | bytes 294928 | tf_op jit(solution)/shard_map/psum | solution.py:282
  721.0 8.7 %fusion.77 = f32[3,16,128]{2,1,0:T(8,128)S(1)} fusion(f32[]{:T(128)} %bitcast.23, f32[8192]{0:T(1024)} %copy-done.76, f32[8192]{0:T(1024)} %copy-done.73, f32[8192]{0:T(1024)} %copy-done.70, f32[8192]{0:T(1024)S(1)} %copy-done.55, s32[8192]{0:T(1024)S(1)} %copy-done.52, s32[128]{0:T(128)} %copy-done.119, f32[8192,3]{0,1:T(4,128)S(1)} %get-tuple-element.123, ...), kind=kOutput, calls=%fused_computation.89 | convolution fusion | flops 618010624 | bytes 811524 | tf_op jit(solution)/shard_map/dot_general | solution.py:101
  729.7 7.8 fusion.87
  737.7 8.1 fusion.67
  747.5 2.5 fusion.31
  751.1 4.5 collective-permute-start.5
  755.6 2.2 collective-permute-done.5
  757.8 5.5 collective-permute-done.4
  764.0 4.4 fusion.414
  768.4 4.1 copy.175
  772.5 3.5 copy.173
  775.9 2.7 collective-permute-start.6
  780.1 5.6 collective-permute-done.7
  785.6 5.6 copy.176
  791.3 5.7 copy.174
  797.0 1.9 maximum_dynamic-update-slice_fusion.5
  803.9 1.9 maximum_dynamic-update-slice_fusion.1
  (377 shorter events, 50.8 us)
Async XLA Ops:
  7.2 192.9 %all-reduce.5.cloned.1.call-start = ((), (), s32[]{:S(2)}) async-start(), calls=%async_computation | async-start | bytes 786432 | tf_op jit(solution)/shard_map/psum | solution.py:270
  16.1 39.8 %copy-start.50 = (s32[8192]{0:T(1024)}, s32[8192]{0:T(1024)S(1)}, u32[]{:S(2)}) copy-start(s32[8192]{0:T(1024)S(1)} %get-tuple-element.159) | copy-start | bytes 98308
  16.3 39.6 %copy-start.53 = (f32[8192]{0:T(1024)}, f32[8192]{0:T(1024)S(1)}, u32[]{:S(2)}) copy-start(f32[8192]{0:T(1024)S(1)} %get-tuple-element.164) | copy-start | bytes 98308
  16.4 315.6 %copy-start.45 = (s32[8192]{0:T(1024)}, s32[8192]{0:T(1024)S(1)}, u32[]{:S(2)}) copy-start(s32[8192]{0:T(1024)S(1)} %get-tuple-element.148) | copy-start | bytes 98308
  16.6 23.0 %copy-start.47 = (f32[8192]{0:T(1024)}, f32[8192]{0:T(1024)S(1)}, u32[]{:S(2)}) copy-start(f32[8192]{0:T(1024)S(1)} %get-tuple-element.153) | copy-start | bytes 98308
  17.0 22.6 %copy-start.60 = (f32[8192]{0:T(1024)}, f32[8192]{0:T(1024)S(1)}, u32[]{:S(2)}) copy-start(f32[8192]{0:T(1024)S(1)} %get-tuple-element.175) | copy-start | bytes 98308
  17.0 38.9 %copy-start.119 = (s32[128]{0:T(128)}, s32[128]{0:T(128)S(1)}, u32[]{:S(2)}) copy-start(s32[128]{0:T(128)S(1)} %iota_add_fusion) | copy-start | bytes 1540
  17.7 38.2 %copy-start.70 = (f32[8192]{0:T(1024)}, f32[8192]{0:T(1024)S(1)}, u32[]{:S(2)}) copy-start(f32[8192]{0:T(1024)S(1)} %get-tuple-element.166) | copy-start | bytes 98308
  17.7 38.2 %copy-start.73 = (f32[8192]{0:T(1024)}, f32[8192]{0:T(1024)S(1)}, u32[]{:S(2)}) copy-start(f32[8192]{0:T(1024)S(1)} %get-tuple-element.167) | copy-start | bytes 98308
  17.7 38.2 %copy-start.76 = (f32[8192]{0:T(1024)}, f32[8192]{0:T(1024)S(1)}, u32[]{:S(2)}) copy-start(f32[8192]{0:T(1024)S(1)} %get-tuple-element.168) | copy-start | bytes 98308
  17.9 21.7 %copy-start.64 = (f32[8192]{0:T(1024)}, f32[8192]{0:T(1024)S(1)}, u32[]{:S(2)}) copy-start(f32[8192]{0:T(1024)S(1)} %get-tuple-element.155) | copy-start | bytes 98308
  17.9 21.7 %copy-start.66 = (f32[8192]{0:T(1024)}, f32[8192]{0:T(1024)S(1)}, u32[]{:S(2)}) copy-start(f32[8192]{0:T(1024)S(1)} %get-tuple-element.156) | copy-start | bytes 98308
  17.9 21.7 %copy-start.68 = (f32[8192]{0:T(1024)}, f32[8192]{0:T(1024)S(1)}, u32[]{:S(2)}) copy-start(f32[8192]{0:T(1024)S(1)} %get-tuple-element.157) | copy-start | bytes 98308
  18.0 21.6 %copy-start.79 = (f32[8192]{0:T(1024)}, f32[8192]{0:T(1024)S(1)}, u32[]{:S(2)}) copy-start(f32[8192]{0:T(1024)S(1)} %get-tuple-element.177) | copy-start | bytes 98308
  18.0 21.6 %copy-start.83 = (f32[8192]{0:T(1024)}, f32[8192]{0:T(1024)S(1)}, u32[]{:S(2)}) copy-start(f32[8192]{0:T(1024)S(1)} %get-tuple-element.178) | copy-start | bytes 98308
  18.0 21.6 %copy-start.87 = (f32[8192]{0:T(1024)}, f32[8192]{0:T(1024)S(1)}, u32[]{:S(2)}) copy-start(f32[8192]{0:T(1024)S(1)} %get-tuple-element.179) | copy-start | bytes 98308
  22.7 317.9 %copy-start.28 = (f32[8192,16]{0,1:T(8,128)}, f32[8192,16]{0,1:T(8,128)S(1)}, u32[]{:S(2)}) copy-start(f32[8192,16]{0,1:T(8,128)S(1)} %select_add_fusion) | copy-start | bytes 1572868
  23.0 309.0 %copy-start.26 = (f32[8192,16]{0,1:T(8,128)}, f32[8192,16]{0,1:T(8,128)S(1)}, u32[]{:S(2)}) copy-start(f32[8192,16]{0,1:T(8,128)S(1)} %select_add_fusion.2) | copy-start | bytes 1572868
  23.2 325.4 %copy-start.31 = (f32[8192,16]{0,1:T(8,128)}, f32[8192,16]{0,1:T(8,128)S(1)}, u32[]{:S(2)}) copy-start(f32[8192,16]{0,1:T(8,128)S(1)} %select_add_fusion.1) | copy-start | bytes 1572868
  56.0 145.6 %copy-start.22 = (f32[1,1,2,3,8192]{4,2,3,1,0:T(2,128)S(1)}, f32[1,1,2,3,8192]{4,2,3,1,0:T(2,128)}, u32[]{:S(2)}) copy-start(f32[1,1,2,3,8192]{4,2,3,1,0:T(2,128)} %param.25) | copy-start | bytes 589828
  56.0 145.8 %copy-start.19 = (f32[1,1,2,8192]{3,2,1,0:T(2,128)S(1)}, f32[1,1,2,8192]{3,2,1,0:T(2,128)}, u32[]{:S(2)}) copy-start(f32[1,1,2,8192]{3,2,1,0:T(2,128)} %param.22) | copy-start | bytes 196612
  56.0 145.8 %copy-start.20 = (f32[1,1,2,8192]{3,2,1,0:T(2,128)S(1)}, f32[1,1,2,8192]{3,2,1,0:T(2,128)}, u32[]{:S(2)}) copy-start(f32[1,1,2,8192]{3,2,1,0:T(2,128)} %param.21) | copy-start | bytes 196612
  56.0 145.8 %copy-start.33 = (f32[1,1,2,8192]{3,2,1,0:T(2,128)S(1)}, f32[1,1,2,8192]{3,2,1,0:T(2,128)}, u32[]{:S(2)}) copy-start(f32[1,1,2,8192]{3,2,1,0:T(2,128)} %param.23) | copy-start | bytes 196612
  72.4 259.5 %copy-start.48 = (f32[8192]{0:T(1024)S(1)}, f32[8192]{0:T(1024)}, u32[]{:S(2)}) copy-start(f32[8192]{0:T(1024)} %copy-done.47) | copy-start | bytes 98308
  73.3 258.7 %copy-start.120 = (s32[128]{0:T(128)S(1)}, s32[128]{0:T(128)}, u32[]{:S(2)}) copy-start(s32[128]{0:T(128)} %copy-done.119) | copy-start | bytes 1540
  73.3 257.5 %all-reduce.7.cloned.1.call-start = ((), (), s32[]{:S(2)}) async-start(), calls=%async_computation.1 | async-start | bytes 786432 | tf_op jit(solution)/shard_map/psum | solution.py:282
  75.9 264.7 %copy-start.43 = (f32[2,3]{0,1:T(4,128)}, f32[2,3]{0,1:T(4,128)S(1)}, u32[]{:S(2)}) copy-start(f32[2,3]{0,1:T(4,128)S(1)} %copy.166) | copy-start | bytes 76
  206.3 382.6 %all-reduce.9.cloned.1.call-start = ((), (), s32[]{:S(2)}) async-start(), calls=%async_computation.2 | async-start | bytes 786432 | tf_op jit(solution)/shard_map/psum | solution.py:270
  207.2 149.8 %copy-start.112 = (f32[16]{0:T(128)}, f32[16]{0:T(128)S(1)}, u32[]{:S(2)}) copy-start(f32[16]{0:T(128)S(1)} %compare_convert_fusion.2) | copy-start | bytes 196
  207.9 149.2 %copy-start.114 = (f32[16]{0:T(128)}, f32[16]{0:T(128)S(1)}, u32[]{:S(2)}) copy-start(f32[16]{0:T(128)S(1)} %compare_convert_fusion) | copy-start | bytes 196
  208.4 148.6 %copy-start.116 = (f32[16]{0:T(128)}, f32[16]{0:T(128)S(1)}, u32[]{:S(2)}) copy-start(f32[16]{0:T(128)S(1)} %compare_convert_fusion.1) | copy-start | bytes 196
  362.1 6.7 collective-permute-start.1
  366.7 7.7 collective-permute-start
  367.3 48.5 %copy-start.35 = (f32[1,16,128]{2,1,0:T(8,128)}, f32[1,16,128]{2,1,0:T(8,128)S(1)}, u32[]{:S(2)}) copy-start(f32[1,16,128]{2,1,0:T(8,128)S(1)} %get-tuple-element.106) | copy-start | bytes 24580
  387.6 15.2 %collective-permute-start.2 = (f32[19,16,18,1]{0,1,3,2:T(8,128)}, f32[19,16,18,1]{0,1,3,2:T(8,128)}, u32[]{:S(2)}, u32[]{:S(2)}) collective-permute-start(f32[19,16,18,1]{0,1,3,2:T(8,128)} %copy.169), channel_id=1, source_target_pairs={{0,1},{1,2},{2,3},{3,4},{4,5},{5,6},{6,7},{7,8},{8,9},{9,10},{10,1... | collective-permute-start | bytes 65672 | tf_op jit(solution)/shard_map/ppermute | solution.py:46
  389.9 7.0 collective-permute-start.3
  390.7 25.1 %copy-start.14 = (f32[15,16,128]{2,1,0:T(8,128)}, f32[15,16,128]{2,1,0:T(8,128)S(1)}, u32[]{:S(2)}) copy-start(f32[15,16,128]{2,1,0:T(8,128)S(1)} %get-tuple-element.85) | copy-start | bytes 368644
  450.5 138.4 %copy-start.44 = (f32[2,3]{0,1:T(4,128)S(1)}, f32[2,3]{0,1:T(4,128)}, u32[]{:S(2)}) copy-start(f32[2,3]{0,1:T(4,128)} %copy-done.43) | copy-start | bytes 76
  450.5 140.0 %copy-start.21 = (f32[1,1,2,8192]{3,2,1,0:T(2,128)S(1)}, f32[1,1,2,8192]{3,2,1,0:T(2,128)}, u32[]{:S(2)}) copy-start(f32[1,1,2,8192]{3,2,1,0:T(2,128)} %param.21) | copy-start | bytes 196612
  450.5 140.0 %copy-start.34 = (f32[1,1,2,8192]{3,2,1,0:T(2,128)S(1)}, f32[1,1,2,8192]{3,2,1,0:T(2,128)}, u32[]{:S(2)}) copy-start(f32[1,1,2,8192]{3,2,1,0:T(2,128)} %param.23) | copy-start | bytes 196612
  450.6 140.0 %copy-start.103 = (f32[2]{0:T(128)S(1)}, f32[2]{0:T(128)}, u32[]{:S(2)}) copy-start(f32[2]{0:T(128)} %get-tuple-element.17) | copy-start | bytes 28
  466.9 128.4 %copy-start.23 = (f32[1,1,2,3,8192]{4,2,3,1,0:T(2,128)S(1)}, f32[1,1,2,3,8192]{4,2,3,1,0:T(2,128)}, u32[]{:S(2)}) copy-start(f32[1,1,2,3,8192]{4,2,3,1,0:T(2,128)} %param.25) | copy-start | bytes 589828
  467.7 252.1 %all-reduce.11.cloned.1.call-start = ((), (), s32[]{:S(2)}) async-start(), calls=%async_computation.3 | async-start | bytes 786432 | tf_op jit(solution)/shard_map/psum | solution.py:282
  750.0 53.1 %copy-start.2 = (f32[19,16,16,128]{3,2,1,0:T(8,128)}, f32[19,16,16,128]{3,2,1,0:T(8,128)S(1)}, u32[]{:S(2)}) copy-start(f32[19,16,16,128]{3,2,1,0:T(8,128)S(1)} %fusion.31) | copy-start | bytes 7471108
  751.1 6.7 collective-permute-start.5
  755.6 7.7 collective-permute-start.4
  775.9 15.3 %collective-permute-start.6 = (f32[19,16,18,1]{0,1,3,2:T(8,128)S(1)}, f32[19,16,18,1]{0,1,3,2:T(8,128)}, u32[]{:S(2)}, u32[]{:S(2)}) collective-permute-start(f32[19,16,18,1]{0,1,3,2:T(8,128)S(1)} %copy.173), channel_id=1, source_target_pairs={{0,1},{1,2},{2,3},{3,4},{4,5},{5,6},{6,7},{7,8},{8,9},{9,10},{10,1... | collective-permute-start | bytes 65672 | tf_op jit(solution)/shard_map/ppermute | solution.py:46
  778.6 7.0 collective-permute-start.7
  (87 other events, 692.4 us)
Sparse Core Ops, SparseCore 0:
  73.4 126.6 all-reduce.4
  206.4 124.3 all-reduce.6
  467.8 121.0 all-reduce.8
  595.4 124.3 all-reduce.10
where the time goes:
time: 827 us; the launch traced here: 819 us
  waiting for transfers between devices  515 us (62%)
  matrix products  147 us (18%)
  local copies, waits for them, and re-layouts  67 us (8%)
  other arithmetic  52.7 us (6%)
  between operations  22.1 us (3%)
  starting transfers between devices  14.5 us (2%)
    psum x2, waiting for transfers between devices, local(): load_rows = lax.psum(row_loads, 'gy')  246 us
    psum x2, waiting for transfers between devices, local(): sampled = lax.psum(samples, 'gy')  244 us
    dot_general x6, matrix products, sample_section(): jnp.dot(across, flattened, precision=lax.Precision.HIGHEST, preferred_ele...  98 us
    dot_general x6, matrix products, spread_section(): lax.dot_general(weighted, across, (((0,), (0,)), ((), ())), precision=lax...  49.3 us
    unnamed x34, other arithmetic  19.7 us
    slice x6, local copies, waits for them, and re-layouts, extended(): lax.slice_in_dim(block, 0, width, axis=dim)  17.4 us
  transfers between devices with their start and end apart: 12, of which 10 were waited for; matrix products, arithmetic and copies ran while one was open for 3% of the time, Pallas kernels for 0%

commit v1 on v0

--- a/solution.py
+++ b/solution.py
@@ -279,7 +279,7 @@
             own_pitch[:, step_index][:, None],
         )
         row_loads = jnp.sum(own_pick[:, :, None, None] * own_loads[:, None], axis=0)
-        load_rows = lax.psum(row_loads, "gy")
+        load_rows = jnp.sum(lax.all_gather(row_loads, "gy"), axis=0)
         force_field = jnp.zeros((3, levels, x_cells, y_cells), jnp.float32)
         for slot_index in range(row_slots):
             section = spread_section(

time: 827 us -> 680 us (0.82)
  waiting for transfers between devices: 515 us -> 357 us
  other arithmetic: 52.7 us -> 64.3 us
    psum x2 -> x0, waiting for transfers between devices: 246 us -> none  [local(): load_rows = lax.psum(row_loads, 'gy')]
    all_gather x0 -> x2, waiting for transfers between devices: none -> 85.6 us  [local(): load_rows = jnp.sum(lax.all_gather(row_loads, 'gy'), axis=0)]
  transfers between devices with their start and end apart: 12 -> 12, of which waited for: 10 -> 10; matrix products, arithmetic and copies ran while one was open for 3% -> 4% of each run, Pallas kernels for 0% -> 0%
where the time goes in v1:
time: 680 us; the launch traced here: 670 us
  waiting for transfers between devices  357 us (52%)
  matrix products  146 us (21%)
  local copies, waits for them, and re-layouts  65.6 us (10%)
  other arithmetic  64.3 us (9%)
  between operations  21.7 us (3%)
  starting transfers between devices  15.7 us (2%)
    psum x2, waiting for transfers between devices, local(): sampled = lax.psum(samples, 'gy')  244 us
    dot_general x6, matrix products, sample_section(): jnp.dot(across, flattened, precision=lax.Precision.HIGHEST, preferred_ele...  98.2 us
    all_gather x2, waiting for transfers between devices, local(): load_rows = jnp.sum(lax.all_gather(row_loads, 'gy'), axis=0)  85.6 us
    dot_general x6, matrix products, spread_section(): lax.dot_general(weighted, across, (((0,), (0,)), ((), ())), precision=lax...  48.2 us
    unnamed x34, other arithmetic  19.7 us
    slice x6, local copies, waits for them, and re-layouts, extended(): lax.slice_in_dim(block, 0, width, axis=dim)  17.5 us
    ppermute x4, waiting for transfers between devices, extended(): lax.ppermute(lax.slice_in_dim(block, 0, width, axis=dim), axis, backward)  16 us
  transfers between devices with their start and end apart: 12, of which 10 were waited for; matrix products, arithmetic and copies ran while one was open for 4% of the time, Pallas kernels for 0%

profile of v1, /device:TPU:27, one launch (start us, length us, event | category | flops | bytes accessed | tf_op | source)
XLA Modules:
  0.0 670.3 jit_solution(5832618063434294344)
XLA Ops:
  22.3 2.4 multiply_reduce_fusion.5
  25.6 16.3 %fusion.50 = f32[8192,3]{0,1:T(4,128)S(1)} fusion(f32[3,16,128]{2,1,0:T(8,128)S(1)} %bitcast.606, f32[]{:T(128)} %bitcast.34, f32[8192]{0:T(1024)S(1)} %get-tuple-element.179, f32[8192]{0:T(1024)S(1)} %get-tuple-element.178, f32[8192]{0:T(1024)S(1)} %get-tuple-element.177, f32[8192]{0:T(1024)S(1)} %get-tuple-element.175, s32[8192]{0:T(1024)S(1)} %get-tuple-element.170, ...), kind=kOutput, calls=%fused_computation.82 | convolution fusion | flops 618373120 | bytes 811524 | tf_op jit(solution)/shard_map/dot_general | solution.py:88
  42.0 16.4 %fusion.44 = f32[8192,3]{0,1:T(4,128)S(1)} fusion(f32[3,16,128]{2,1,0:T(8,128)S(1)} %bitcast.605, f32[]{:T(128)} %bitcast.8, f32[8192]{0:T(1024)S(1)} %get-tuple-element.157, f32[8192]{0:T(1024)S(1)} %get-tuple-element.156, f32[8192]{0:T(1024)S(1)} %get-tuple-element.155, f32[8192]{0:T(1024)S(1)} %get-tuple-element.153, s32[8192]{0:T(1024)S(1)} %get-tuple-element.148, ...), kind=kOutput, calls=%fused_computation.80 | convolution fusion | flops 618373120 | bytes 811524 | tf_op jit(solution)/shard_map/dot_general | solution.py:88
  58.6 16.4 %fusion.47 = f32[8192,3]{0,1:T(4,128)S(1)} fusion(f32[3,16,128]{2,1,0:T(8,128)S(1)} %bitcast.604, f32[]{:T(128)} %bitcast.23, f32[8192]{0:T(1024)S(1)} %copy-done.81, f32[8192]{0:T(1024)S(1)} %copy-done.77, f32[8192]{0:T(1024)S(1)} %copy-done.73, f32[8192]{0:T(1024)S(1)} %copy-done.53, s32[8192]{0:T(1024)S(1)} %copy-done.51, s32[128]{0:T(128)S(1)} %copy-done.130, ...), kind=kOutput, calls=%fused_computation.81 | convolution fusion | flops 618373120 | bytes 811524 | tf_op jit(solution)/shard_map/dot_general | solution.py:88
  79.6 123.1 %all-reduce.3.cloned.1.call-done = f32[3,3,8192]{2,1,0:T(4,128)} async-done(((f32[3,3,8192]{2,1,0:T(4,128)}), f32[3,3,8192]{2,1,0:T(4,128)}) %all-reduce.3.cloned.1.call-update) | async-done | bytes 294928 | tf_op jit(solution)/shard_map/psum | solution.py:270
  207.2 1.6 multiply_reduce_fusion.8
  211.7 41.9 %all-gather.5.cloned.1.call-done = f32[48,3,8192]{2,1,0:T(4,128)} async-done(((f32[3,3,8192]{2,1,0:T(4,128)}), f32[48,3,8192]{2,1,0:T(4,128)}) %all-gather.5.cloned.1.call-update) | async-done | bytes 4718608 | tf_op jit(solution)/shard_map/all_gather | solution.py:282
  253.7 4.0 reduce_sum.560
  257.9 8.4 %fusion.62 = f32[3,16,128]{2,1,0:T(8,128)S(1)} fusion(f32[]{:T(128)} %bitcast.8, f32[8192]{0:T(1024)S(1)} %copy-done.71, f32[8192]{0:T(1024)S(1)} %copy-done.68, f32[8192]{0:T(1024)S(1)} %copy-done.65, f32[8192]{0:T(1024)S(1)} %copy-done.49, s32[8192]{0:T(1024)S(1)} %get-tuple-element.148, s32[128]{0:T(128)S(1)} %copy-done.130, ...), kind=kOutput, calls=%fused_computation.86 | convolution fusion | flops 618010624 | bytes 811524 | tf_op jit(solution)/shard_map/dot_general | solution.py:101
  266.4 7.9 %fusion.82 = f32[3,16,128]{2,1,0:T(8,128)S(1)} fusion(f32[]{:T(128)} %bitcast.34, f32[8192]{0:T(1024)S(1)} %copy-done.94, f32[8192]{0:T(1024)S(1)} %copy-done.90, f32[8192]{0:T(1024)S(1)} %copy-done.86, f32[8192]{0:T(1024)S(1)} %copy-done.61, s32[8192]{0:T(1024)S(1)} %copy-done.57, s32[128]{0:T(128)S(1)} %copy-done.131, ...), kind=kOutput, calls=%fused_computation.90 | convolution fusion | flops 618010624 | bytes 811524 | tf_op jit(solution)/shard_map/dot_general | solution.py:101
  274.4 8.0 %fusion.72 = f32[3,16,128]{2,1,0:T(8,128)S(1)} fusion(f32[]{:T(128)} %bitcast.23, f32[8192]{0:T(1024)S(1)} %copy-done.82, f32[8192]{0:T(1024)S(1)} %copy-done.78, f32[8192]{0:T(1024)S(1)} %copy-done.74, f32[8192]{0:T(1024)S(1)} %copy-done.54, s32[8192]{0:T(1024)S(1)} %copy-done.51, s32[128]{0:T(128)S(1)} %copy-done.131, ...), kind=kOutput, calls=%fused_computation.88 | convolution fusion | flops 618010624 | bytes 811524 | tf_op jit(solution)/shard_map/dot_general | solution.py:101
  284.2 2.5 fusion.24
  287.6 4.5 collective-permute-start.1
  292.8 2.5 collective-permute-done.1
  295.3 5.5 collective-permute-done
  301.4 4.5 fusion.415
  305.9 4.1 copy.171
  310.0 4.1 copy.169
  314.1 3.1 collective-permute-start.2
  319.4 4.8 collective-permute-done.3
  324.1 5.9 copy.172
  330.1 5.7 copy.170
  335.8 1.9 constant_dynamic-update-slice_fusion.5
  344.9 16.4 %fusion.59 = f32[8192,3]{0,1:T(4,128)S(1)} fusion(f32[3,16,128]{2,1,0:T(8,128)S(1)} %bitcast.609, f32[]{:T(128)} %bitcast.34, f32[8192]{0:T(1024)S(1)} %copy-done.95, f32[8192]{0:T(1024)S(1)} %copy-done.91, f32[8192]{0:T(1024)S(1)} %copy-done.87, f32[8192]{0:T(1024)S(1)} %copy-done.62, s32[8192]{0:T(1024)S(1)} %copy-done.58, s32[128]{0:T(128)S(1)} %copy-done.132, ...), kind=kOutput, calls=%fused_computation.85 | convolution fusion | flops 618373120 | bytes 811524 | tf_op jit(solution)/shard_map/dot_general | solution.py:88
  361.4 16.4 %fusion.56 = f32[8192,3]{0,1:T(4,128)S(1)} fusion(f32[3,16,128]{2,1,0:T(8,128)S(1)} %bitcast.608, f32[]{:T(128)} %bitcast.23, f32[8192]{0:T(1024)S(1)} %copy-done.83, f32[8192]{0:T(1024)S(1)} %copy-done.79, f32[8192]{0:T(1024)S(1)} %copy-done.75, f32[8192]{0:T(1024)S(1)} %copy-done.55, s32[8192]{0:T(1024)S(1)} %copy-done.52, s32[128]{0:T(128)S(1)} %copy-done.132, ...), kind=kOutput, calls=%fused_computation.84 | convolution fusion | flops 618373120 | bytes 811524 | tf_op jit(solution)/shard_map/dot_general | solution.py:88
  377.9 16.4 %fusion.53 = f32[8192,3]{0,1:T(4,128)S(1)} fusion(f32[3,16,128]{2,1,0:T(8,128)S(1)} %bitcast.607, f32[]{:T(128)} %bitcast.8, f32[8192]{0:T(1024)S(1)} %copy-done.72, f32[8192]{0:T(1024)S(1)} %copy-done.69, f32[8192]{0:T(1024)S(1)} %copy-done.66, f32[8192]{0:T(1024)S(1)} %copy-done.50, s32[8192]{0:T(1024)S(1)} %copy-done.47, s32[128]{0:T(128)S(1)} %copy-done.132, ...), kind=kOutput, calls=%fused_computation.83 | convolution fusion | flops 618373120 | bytes 811524 | tf_op jit(solution)/shard_map/dot_general | solution.py:88
  395.2 120.8 %all-reduce.5.cloned.1.call-done = f32[3,3,8192]{2,1,0:T(4,128)} async-done(((f32[3,3,8192]{2,1,0:T(4,128)}), f32[3,3,8192]{2,1,0:T(4,128)}) %all-reduce.5.cloned.1.call-update) | async-done | bytes 294928 | tf_op jit(solution)/shard_map/psum | solution.py:270
  516.0 1.5 multiply_reduce_fusion.7
  517.6 1.8 add_multiply_fusion.15
  520.9 1.6 multiply_reduce_fusion.6
  523.7 43.7 %all-gather.7.cloned.1.call-done = f32[48,3,8192]{2,1,0:T(4,128)} async-done(((f32[3,3,8192]{2,1,0:T(4,128)}), f32[48,3,8192]{2,1,0:T(4,128)}) %all-gather.7.cloned.1.call-update) | async-done | bytes 4718608 | tf_op jit(solution)/shard_map/all_gather | solution.py:282
  567.4 4.0 reduce_sum.596
  571.6 7.9 %fusion.77 = f32[3,16,128]{2,1,0:T(8,128)S(1)} fusion(f32[]{:T(128)} %bitcast.23, f32[8192]{0:T(1024)S(1)} %copy-done.84, f32[8192]{0:T(1024)S(1)} %copy-done.80, f32[8192]{0:T(1024)S(1)} %copy-done.76, f32[8192]{0:T(1024)S(1)} %copy-done.55, s32[8192]{0:T(1024)S(1)} %copy-done.52, s32[128]{0:T(128)S(1)} %copy-done.133, ...), kind=kOutput, calls=%fused_computation.89 | convolution fusion | flops 618010624 | bytes 811524 | tf_op jit(solution)/shard_map/dot_general | solution.py:101
  579.6 7.8 %fusion.87 = f32[3,16,128]{2,1,0:T(8,128)S(1)} fusion(f32[]{:T(128)} %bitcast.34, f32[8192]{0:T(1024)S(1)} %copy-done.96, f32[8192]{0:T(1024)S(1)} %copy-done.92, f32[8192]{0:T(1024)S(1)} %copy-done.88, f32[8192]{0:T(1024)S(1)} %copy-done.63, s32[8192]{0:T(1024)S(1)} %copy-done.59, s32[128]{0:T(128)S(1)} %copy-done.133, ...), kind=kOutput, calls=%fused_computation.91 | convolution fusion | flops 618010624 | bytes 811524 | tf_op jit(solution)/shard_map/dot_general | solution.py:101
  587.5 8.1 %fusion.67 = f32[3,16,128]{2,1,0:T(8,128)S(1)} fusion(f32[]{:T(128)} %bitcast.8, f32[8192]{0:T(1024)S(1)} %copy-done.72, f32[8192]{0:T(1024)S(1)} %copy-done.69, f32[8192]{0:T(1024)S(1)} %copy-done.66, f32[8192]{0:T(1024)S(1)} %copy-done.50, s32[8192]{0:T(1024)S(1)} %copy-done.47, s32[128]{0:T(128)S(1)} %copy-done.133, ...), kind=kOutput, calls=%fused_computation.87 | convolution fusion | flops 618010624 | bytes 811524 | tf_op jit(solution)/shard_map/dot_general | solution.py:101
  597.4 2.5 fusion.31
  601.0 4.5 collective-permute-start.5
  605.6 3.1 collective-permute-done.5
  608.7 5.5 collective-permute-done.4
  614.8 4.5 fusion.414
  619.3 4.1 copy.175
  623.4 3.5 copy.173
  626.9 3.3 collective-permute-start.6
  631.6 5.6 collective-permute-done.7
  637.2 5.7 copy.176
  642.9 5.7 copy.174
  648.6 1.9 maximum_dynamic-update-slice_fusion.5
  655.5 1.9 maximum_dynamic-update-slice_fusion.1
  (401 shorter events, 55.1 us)
Async XLA Ops:
  7.2 195.5 %all-reduce.3.cloned.1.call-start = ((), (), s32[]{:S(2)}) async-start(), calls=%async_computation | async-start | bytes 786432 | tf_op jit(solution)/shard_map/psum | solution.py:270
  17.6 240.2 %copy-start.46 = (s32[8192]{0:T(1024)}, s32[8192]{0:T(1024)S(1)}, u32[]{:S(2)}) copy-start(s32[8192]{0:T(1024)S(1)} %get-tuple-element.148) | copy-start | bytes 98308
  17.9 24.1 %copy-start.48 = (f32[8192]{0:T(1024)}, f32[8192]{0:T(1024)S(1)}, u32[]{:S(2)}) copy-start(f32[8192]{0:T(1024)S(1)} %get-tuple-element.153) | copy-start | bytes 98308
  18.2 23.7 %copy-start.60 = (f32[8192]{0:T(1024)}, f32[8192]{0:T(1024)S(1)}, u32[]{:S(2)}) copy-start(f32[8192]{0:T(1024)S(1)} %get-tuple-element.175) | copy-start | bytes 98308
  20.2 21.7 %copy-start.64 = (f32[8192]{0:T(1024)}, f32[8192]{0:T(1024)S(1)}, u32[]{:S(2)}) copy-start(f32[8192]{0:T(1024)S(1)} %get-tuple-element.155) | copy-start | bytes 98308
  20.3 21.7 %copy-start.67 = (f32[8192]{0:T(1024)}, f32[8192]{0:T(1024)S(1)}, u32[]{:S(2)}) copy-start(f32[8192]{0:T(1024)S(1)} %get-tuple-element.156) | copy-start | bytes 98308
  20.3 21.7 %copy-start.70 = (f32[8192]{0:T(1024)}, f32[8192]{0:T(1024)S(1)}, u32[]{:S(2)}) copy-start(f32[8192]{0:T(1024)S(1)} %get-tuple-element.157) | copy-start | bytes 98308
  20.4 21.5 %copy-start.85 = (f32[8192]{0:T(1024)}, f32[8192]{0:T(1024)S(1)}, u32[]{:S(2)}) copy-start(f32[8192]{0:T(1024)S(1)} %get-tuple-element.177) | copy-start | bytes 98308
  20.4 21.5 %copy-start.89 = (f32[8192]{0:T(1024)}, f32[8192]{0:T(1024)S(1)}, u32[]{:S(2)}) copy-start(f32[8192]{0:T(1024)S(1)} %get-tuple-element.178) | copy-start | bytes 98308
  20.4 21.5 %copy-start.93 = (f32[8192]{0:T(1024)}, f32[8192]{0:T(1024)S(1)}, u32[]{:S(2)}) copy-start(f32[8192]{0:T(1024)S(1)} %get-tuple-element.179) | copy-start | bytes 98308
  25.1 241.2 %copy-start.28 = (f32[8192,16]{0,1:T(8,128)}, f32[8192,16]{0,1:T(8,128)S(1)}, u32[]{:S(2)}) copy-start(f32[8192,16]{0,1:T(8,128)S(1)} %select_add_fusion) | copy-start | bytes 1572868
  25.3 232.5 %copy-start.26 = (f32[8192,16]{0,1:T(8,128)}, f32[8192,16]{0,1:T(8,128)S(1)}, u32[]{:S(2)}) copy-start(f32[8192,16]{0,1:T(8,128)S(1)} %select_add_fusion.2) | copy-start | bytes 1572868
  25.5 32.9 %copy-start.31 = (f32[8192,16]{0,1:T(8,128)}, f32[8192,16]{0,1:T(8,128)S(1)}, u32[]{:S(2)}) copy-start(f32[8192,16]{0,1:T(8,128)S(1)} %select_add_fusion.1) | copy-start | bytes 1572868
  42.0 16.5 %copy-start.51 = (s32[8192]{0:T(1024)S(1)}, s32[8192]{0:T(1024)}, u32[]{:S(2)}) copy-start(s32[8192]{0:T(1024)} %get-tuple-element.159) | copy-start | bytes 98308
  42.0 16.5 %copy-start.53 = (f32[8192]{0:T(1024)S(1)}, f32[8192]{0:T(1024)}, u32[]{:S(2)}) copy-start(f32[8192]{0:T(1024)} %get-tuple-element.164) | copy-start | bytes 98308
  58.5 18.2 %copy-start.119 = (s32[3]{0:T(128)S(1)}, s32[3]{0:T(128)}, u32[]{:S(2)}) copy-start(s32[3]{0:T(128)} %copy-done.118) | copy-start | bytes 40
  58.5 18.2 %copy-start.128 = (s32[40,2]{0,1:T(2,128)S(1)}, s32[40,2]{0,1:T(2,128)}, u32[]{:S(2)}) copy-start(s32[40,2]{0,1:T(2,128)} %param.20) | copy-start | bytes 964
  58.5 19.1 %copy-start.43 = (f32[1,1,2,8192]{3,2,1,0:T(2,128)S(1)}, f32[1,1,2,8192]{3,2,1,0:T(2,128)}, u32[]{:S(2)}) copy-start(f32[1,1,2,8192]{3,2,1,0:T(2,128)} %param.24) | copy-start | bytes 196612
  58.5 20.0 %copy-start.120 = (s32[3]{0:T(128)S(1)}, s32[3]{0:T(128)}, u32[]{:S(2)}) copy-start(s32[3]{0:T(128)} %get-tuple-element.61) | copy-start | bytes 40
  58.5 145.6 %copy-start.22 = (f32[1,1,2,3,8192]{4,2,3,1,0:T(2,128)S(1)}, f32[1,1,2,3,8192]{4,2,3,1,0:T(2,128)}, u32[]{:S(2)}) copy-start(f32[1,1,2,3,8192]{4,2,3,1,0:T(2,128)} %param.25) | copy-start | bytes 589828
  58.6 145.8 %copy-start.19 = (f32[1,1,2,8192]{3,2,1,0:T(2,128)S(1)}, f32[1,1,2,8192]{3,2,1,0:T(2,128)}, u32[]{:S(2)}) copy-start(f32[1,1,2,8192]{3,2,1,0:T(2,128)} %param.22) | copy-start | bytes 196612
  58.6 145.8 %copy-start.20 = (f32[1,1,2,8192]{3,2,1,0:T(2,128)S(1)}, f32[1,1,2,8192]{3,2,1,0:T(2,128)}, u32[]{:S(2)}) copy-start(f32[1,1,2,8192]{3,2,1,0:T(2,128)} %param.21) | copy-start | bytes 196612
  58.6 145.8 %copy-start.34 = (f32[1,1,2,8192]{3,2,1,0:T(2,128)S(1)}, f32[1,1,2,8192]{3,2,1,0:T(2,128)}, u32[]{:S(2)}) copy-start(f32[1,1,2,8192]{3,2,1,0:T(2,128)} %param.23) | copy-start | bytes 196612
  75.9 177.8 %all-gather.5.cloned.1.call-start = ((), (), s32[]{:S(2)}) async-start(), calls=%async_computation.2 | async-start | bytes 6684672 | tf_op jit(solution)/shard_map/all_gather | solution.py:282
  78.7 179.0 %copy-start.44 = (f32[2,3]{0,1:T(4,128)}, f32[2,3]{0,1:T(4,128)S(1)}, u32[]{:S(2)}) copy-start(f32[2,3]{0,1:T(4,128)S(1)} %copy.166) | copy-start | bytes 76
  208.8 307.2 %all-reduce.5.cloned.1.call-start = ((), (), s32[]{:S(2)}) async-start(), calls=%async_computation.1 | async-start | bytes 786432 | tf_op jit(solution)/shard_map/psum | solution.py:270
  209.4 73.1 %copy-start.122 = (f32[16]{0:T(128)}, f32[16]{0:T(128)S(1)}, u32[]{:S(2)}) copy-start(f32[16]{0:T(128)S(1)} %compare_convert_fusion.2) | copy-start | bytes 196
  287.6 7.7 %collective-permute-start.1 = (f32[19,16,1,128]{3,2,1,0:T(1,128)S(1)}, f32[19,16,1,128]{3,2,1,0:T(1,128)S(1)}, u32[]{:S(2)}, u32[]{:S(2)}) collective-permute-start(f32[19,16,1,128]{3,2,1,0:T(1,128)S(1)} %get-tuple-element.115), channel_id=1, source_target_pairs={{16,0},{32,16},{48,32},{64,48},{80,64},{96,80},{112,96},{128,112},... | collective-permute-start | bytes 466952 | tf_op jit(solution)/shard_map/ppermute | solution.py:49
  292.2 8.6 %collective-permute-start = (f32[19,16,1,128]{3,2,1,0:T(1,128)S(1)}, f32[19,16,1,128]{3,2,1,0:T(1,128)S(1)}, u32[]{:S(2)}, u32[]{:S(2)}) collective-permute-start(f32[19,16,1,128]{3,2,1,0:T(1,128)S(1)} %get-tuple-element.116), channel_id=1, source_target_pairs={{0,16},{16,32},{32,48},{48,64},{64,80},{80,96},{96,112},{112,128},... | collective-permute-start | bytes 466952 | tf_op jit(solution)/shard_map/ppermute | solution.py:46
  292.8 50.3 %copy-start.36 = (f32[1,16,128]{2,1,0:T(8,128)}, f32[1,16,128]{2,1,0:T(8,128)S(1)}, u32[]{:S(2)}) copy-start(f32[1,16,128]{2,1,0:T(8,128)S(1)} %get-tuple-element.106) | copy-start | bytes 24580
  314.1 16.0 %collective-permute-start.2 = (f32[19,16,18,1]{0,1,3,2:T(8,128)}, f32[19,16,18,1]{0,1,3,2:T(8,128)}, u32[]{:S(2)}, u32[]{:S(2)}) collective-permute-start(f32[19,16,18,1]{0,1,3,2:T(8,128)} %copy.169), channel_id=1, source_target_pairs={{0,1},{1,2},{2,3},{3,4},{4,5},{5,6},{6,7},{7,8},{8,9},{9,10},{10,1... | collective-permute-start | bytes 65672 | tf_op jit(solution)/shard_map/ppermute | solution.py:46
  317.2 7.0 %collective-permute-start.3 = (f32[19,16,18,1]{0,1,3,2:T(8,128)}, f32[19,16,18,1]{0,1,3,2:T(8,128)}, u32[]{:S(2)}, u32[]{:S(2)}) collective-permute-start(f32[19,16,18,1]{0,1,3,2:T(8,128)} %copy.171), channel_id=1, source_target_pairs={{1,0},{2,1},{3,2},{4,3},{5,4},{6,5},{7,6},{8,7},{9,8},{10,9},{11,1... | collective-permute-start | bytes 65672 | tf_op jit(solution)/shard_map/ppermute | solution.py:49
  317.9 25.2 %copy-start.14 = (f32[15,16,128]{2,1,0:T(8,128)}, f32[15,16,128]{2,1,0:T(8,128)S(1)}, u32[]{:S(2)}) copy-start(f32[15,16,128]{2,1,0:T(8,128)S(1)} %get-tuple-element.85) | copy-start | bytes 368644
  343.3 18.0 %copy-start.9 = (f32[19,16,16,128]{3,2,1,0:T(8,128)}, f32[19,16,16,128]{3,2,1,0:T(8,128)S(1)}, u32[]{:S(2)}) copy-start(f32[19,16,16,128]{3,2,1,0:T(8,128)S(1)} %fusion.145) | copy-start | bytes 7471108
  343.9 17.3 %copy-start.12 = (f32[16,16,128]{2,1,0:T(8,128)}, f32[16,16,128]{2,1,0:T(8,128)S(1)}, u32[]{:S(2)}) copy-start(f32[16,16,128]{2,1,0:T(8,128)S(1)} %get-tuple-element.12) | copy-start | bytes 393220
  377.8 138.2 %copy-start.45 = (f32[2,3]{0,1:T(4,128)S(1)}, f32[2,3]{0,1:T(4,128)}, u32[]{:S(2)}) copy-start(f32[2,3]{0,1:T(4,128)} %copy-done.44) | copy-start | bytes 76
  377.8 139.8 %copy-start.21 = (f32[1,1,2,8192]{3,2,1,0:T(2,128)S(1)}, f32[1,1,2,8192]{3,2,1,0:T(2,128)}, u32[]{:S(2)}) copy-start(f32[1,1,2,8192]{3,2,1,0:T(2,128)} %param.21) | copy-start | bytes 196612
  377.8 139.8 %copy-start.35 = (f32[1,1,2,8192]{3,2,1,0:T(2,128)S(1)}, f32[1,1,2,8192]{3,2,1,0:T(2,128)}, u32[]{:S(2)}) copy-start(f32[1,1,2,8192]{3,2,1,0:T(2,128)} %param.23) | copy-start | bytes 196612
  377.9 139.8 %copy-start.111 = (f32[2]{0:T(128)S(1)}, f32[2]{0:T(128)}, u32[]{:S(2)}) copy-start(f32[2]{0:T(128)} %get-tuple-element.17) | copy-start | bytes 28
  394.3 128.3 %copy-start.117 = (pred[3]{0:T(512)(128)(4,1)S(1)}, pred[3]{0:T(512)(128)(4,1)}, u32[]{:S(2)}) copy-start(pred[3]{0:T(512)(128)(4,1)} %copy-done.116) | copy-start | bytes 13
  394.3 128.3 %copy-start.121 = (s32[3]{0:T(128)S(1)}, s32[3]{0:T(128)}, u32[]{:S(2)}) copy-start(s32[3]{0:T(128)} %get-tuple-element.61) | copy-start | bytes 40
  394.3 128.4 %copy-start.23 = (f32[1,1,2,3,8192]{4,2,3,1,0:T(2,128)S(1)}, f32[1,1,2,3,8192]{4,2,3,1,0:T(2,128)}, u32[]{:S(2)}) copy-start(f32[1,1,2,3,8192]{4,2,3,1,0:T(2,128)} %param.25) | copy-start | bytes 589828
  395.2 172.2 %all-gather.7.cloned.1.call-start = ((), (), s32[]{:S(2)}) async-start(), calls=%async_computation.3 | async-start | bytes 6684672 | tf_op jit(solution)/shard_map/all_gather | solution.py:282
  599.9 54.8 %copy-start.2 = (f32[19,16,16,128]{3,2,1,0:T(8,128)}, f32[19,16,16,128]{3,2,1,0:T(8,128)S(1)}, u32[]{:S(2)}) copy-start(f32[19,16,16,128]{3,2,1,0:T(8,128)S(1)} %fusion.31) | copy-start | bytes 7471108
  601.0 7.7 %collective-permute-start.5 = (f32[19,16,1,128]{3,2,1,0:T(1,128)S(1)}, f32[19,16,1,128]{3,2,1,0:T(1,128)S(1)}, u32[]{:S(2)}, u32[]{:S(2)}) collective-permute-start(f32[19,16,1,128]{3,2,1,0:T(1,128)S(1)} %get-tuple-element.100), channel_id=1, source_target_pairs={{16,0},{32,16},{48,32},{64,48},{80,64},{96,80},{112,96},{128,112},... | collective-permute-start | bytes 466952 | tf_op jit(solution)/shard_map/ppermute | solution.py:49
  605.6 8.6 %collective-permute-start.4 = (f32[19,16,1,128]{3,2,1,0:T(1,128)S(1)}, f32[19,16,1,128]{3,2,1,0:T(1,128)S(1)}, u32[]{:S(2)}, u32[]{:S(2)}) collective-permute-start(f32[19,16,1,128]{3,2,1,0:T(1,128)S(1)} %get-tuple-element.101), channel_id=1, source_target_pairs={{0,16},{16,32},{32,48},{48,64},{64,80},{80,96},{96,112},{112,128},... | collective-permute-start | bytes 466952 | tf_op jit(solution)/shard_map/ppermute | solution.py:46
  626.9 16.0 %collective-permute-start.6 = (f32[19,16,18,1]{0,1,3,2:T(8,128)S(1)}, f32[19,16,18,1]{0,1,3,2:T(8,128)}, u32[]{:S(2)}, u32[]{:S(2)}) collective-permute-start(f32[19,16,18,1]{0,1,3,2:T(8,128)S(1)} %copy.173), channel_id=1, source_target_pairs={{0,1},{1,2},{2,3},{3,4},{4,5},{5,6},{6,7},{7,8},{8,9},{9,10},{10,1... | collective-permute-start | bytes 65672 | tf_op jit(solution)/shard_map/ppermute | solution.py:46
  630.2 7.0 %collective-permute-start.7 = (f32[19,16,18,1]{0,1,3,2:T(8,128)}, f32[19,16,18,1]{0,1,3,2:T(8,128)}, u32[]{:S(2)}, u32[]{:S(2)}) collective-permute-start(f32[19,16,18,1]{0,1,3,2:T(8,128)} %copy.175), channel_id=1, source_target_pairs={{1,0},{2,1},{3,2},{4,3},{5,4},{6,5},{7,6},{8,7},{9,8},{10,9},{11,1... | collective-permute-start | bytes 65672 | tf_op jit(solution)/shard_map/ppermute | solution.py:49
  (98 other events, 723.3 us)
Sparse Core Ops, SparseCore 0:
  76.0 126.6 all-reduce.2
  209.0 44.6 all-gather.4
  395.3 120.6 all-reduce.4
  522.7 44.6 all-gather.6
